TPU v7x, 128 devices: a whole 4x4x4 slice. The times are simulated.
128 devices in a mesh: enc: 8 (over z, core), gen: 16 (over x, y).
Axes of the slice: x: 4, y: 4, z: 4, core: 2. Of those that a mesh axis runs over, the one named last changes fastest.
Arguments:
- hidden_states: bfloat16 [8192, 4096], P('gen'), may hold values from -60 to 60
- grad_out: bfloat16 [8192, 4096], P('gen'), may hold values from -0.29882812 to 0.29882812
- nbr_embed: bfloat16 [256, 128, 1024], P(('enc', 'gen')), may hold values from -60 to 60
- nbr_index: int32 [128, 2], replicated, may hold values from 0 to 255, as said below
- gain: float32 [4096], replicated, may hold values from 0.5 to 1.5
- w_query: bfloat16 [4096, 4096], P(None, 'enc'), may hold values from -0.1875 to 0.1875
- w_out: bfloat16 [4096, 4096], P('enc'), may hold values from -0.09375 to 0.09375
- w_key: bfloat16 [1024, 4096], P(None, 'enc'), may hold values from -0.1875 to 0.1875
- w_value: bfloat16 [1024, 4096], P(None, 'enc'), may hold values from -0.75 to 0.75
- enc_gain: float32 [1024], replicated, may hold values from 0.5 to 1.5
- enc_qkv: bfloat16 [1024, 3072], replicated, may hold values from -0.1875 to 0.1875
- enc_out: bfloat16 [1024, 1024], replicated, may hold values from -0.1875 to 0.1875
Outputs:
- grad_encoded: float32 [256, 128, 1024], P(('enc', 'gen'))
- grad_w_out: float32 [4096, 4096], P('enc', 'gen')
- grad_w_key: float32 [1024, 4096], P('gen', 'enc')
- grad_w_value: float32 [1024, 4096], P('gen', 'enc')
Inputs may be any that keep to these rules, and one draw needn't show every extreme that they name: `nbr_index`: every entry 0 to 255 is named exactly once. Entry p is held by index (p // 2) % 16 of gen; block c belongs to index c * 64 // 512 of gen. The blocks of one index of gen name at most 2 entries held by one index of gen, and some pair of indices reaches 2 in every draw.
All inputs are finite; a program needn't handle non-finite values.
Results may differ from a plain program's by a relative error of at most 0.038.
Values may be sent and summed in bfloat16 or wider, within the bound.
A program may use at most 128 MiB of HBM per device.

v0:
```python
import jax
import jax.numpy as jnp
from jax import lax
from jax.sharding import PartitionSpec as P

H = 32
EH = 8
CH = 64
K = 2
SOFTCAP = 5.0
EPSILON = 1e-06


def rms_scale(values, gain):
    wide = values.astype(jnp.float32)
    factor = lax.rsqrt(jnp.mean(wide * wide, axis=-1, keepdims=True) + EPSILON)
    return (wide * factor * gain).astype(jnp.bfloat16)


def attention_parts(queries, keys_all, values_all):
    head_width = queries.shape[-1]
    raw_scores = jnp.einsum(
        "bqhd,bkhd->bhqk", queries, keys_all, preferred_element_type=jnp.float32
    ) * head_width ** (-0.5)
    capped = SOFTCAP * jnp.tanh(raw_scores / SOFTCAP)
    expo_terms = jnp.exp(capped)
    probs_full = expo_terms / jnp.sum(expo_terms, axis=-1, keepdims=True)
    probs_low = probs_full.astype(jnp.bfloat16)
    mixed = jnp.einsum(
        "bhqk,bkhd->bqhd", probs_low, values_all, preferred_element_type=jnp.float32
    ).astype(jnp.bfloat16)
    return (raw_scores, probs_full, probs_low, mixed)


def attention_grads(queries, values_all, raw_scores, probs_full, probs_low, d_mixed):
    head_width = queries.shape[-1]
    d_probs = jnp.einsum("bqhd,bkhd->bhqk", d_mixed, values_all, preferred_element_type=jnp.float32)
    d_capped = probs_full * (d_probs - jnp.sum(probs_full * d_probs, axis=-1, keepdims=True))
    slope = jnp.tanh(raw_scores / SOFTCAP)
    d_raw = (d_capped * (1.0 - slope * slope) * head_width ** (-0.5)).astype(jnp.bfloat16)
    d_keys = jnp.einsum(
        "bhqk,bqhd->bkhd", d_raw, queries, preferred_element_type=jnp.float32
    ).astype(jnp.bfloat16)
    d_values = jnp.einsum(
        "bhqk,bqhd->bkhd", probs_low, d_mixed, preferred_element_type=jnp.float32
    ).astype(jnp.bfloat16)
    return (d_keys, d_values)


def encode(nbr_embed, enc_gain, enc_qkv, enc_out):
    entries, length, enc_width = nbr_embed.shape
    normed = rms_scale(nbr_embed, enc_gain).reshape(entries * length, enc_width)
    projected = jnp.dot(normed, enc_qkv, preferred_element_type=jnp.float32).astype(jnp.bfloat16)
    projected = projected.reshape(entries, length, 3, EH, enc_width // EH)
    outputs = attention_parts(projected[:, :, 0], projected[:, :, 1], projected[:, :, 2])
    attended = outputs[3].reshape(entries * length, enc_width)
    update = jnp.dot(attended, enc_out, preferred_element_type=jnp.float32).reshape(
        entries, length, enc_width
    )
    return (nbr_embed.astype(jnp.float32) + update).astype(jnp.bfloat16)


def routing(nbr_index, row_index, gen_count, per_device, row_size, capacity):
    slot_entries = nbr_index.reshape(-1)
    entry_count = slot_entries.shape[0]
    slot_ids = jnp.arange(entry_count, dtype=jnp.int32)
    target = slot_ids // row_size
    source = slot_entries // per_device % gen_count
    column = slot_entries // (per_device * gen_count) * per_device + slot_entries % per_device
    pair_ids = target * gen_count + source
    pair_onehot = (
        pair_ids[:, None] == jnp.arange(gen_count * gen_count, dtype=jnp.int32)[None, :]
    ).astype(jnp.int32)
    earlier = jnp.cumsum(pair_onehot, axis=0) - pair_onehot
    rank_in = jnp.sum(earlier * pair_onehot, axis=1)
    send_slot = target * capacity + rank_in
    buffer_ids = jnp.arange(gen_count * capacity, dtype=jnp.int32)
    is_mine = (source == row_index).astype(jnp.int32)
    send_match = (send_slot[:, None] == buffer_ids[None, :]).astype(jnp.int32) * is_mine[:, None]
    send_column = jnp.sum(send_match * column[:, None], axis=0)
    column_ids = jnp.arange(row_size, dtype=jnp.int32)
    column_match = (column[:, None] == column_ids[None, :]).astype(jnp.int32) * is_mine[:, None]
    column_position = jnp.sum(column_match * send_slot[:, None], axis=0)
    own_source = lax.dynamic_slice_in_dim(source, row_index * row_size, row_size)
    own_rank = lax.dynamic_slice_in_dim(rank_in, row_index * row_size, row_size)
    receive_position = own_source * capacity + own_rank
    receive_match = (receive_position[:, None] == buffer_ids[None, :]).astype(jnp.int32)
    position_slot = jnp.sum(receive_match * column_ids[:, None], axis=0)
    return (send_column, column_position, receive_position, position_slot)


def local(
    hidden_states,
    grad_out,
    nbr_embed,
    nbr_index,
    gain,
    w_query,
    w_out,
    w_key,
    w_value,
    enc_gain,
    enc_qkv,
    enc_out,
):
    enc_count = lax.axis_size("enc")
    gen_count = lax.axis_size("gen")
    row_index = lax.axis_index("gen")
    per_device, length, enc_width = nbr_embed.shape
    row_size = per_device * enc_count
    capacity = max(2, 2 * row_size // gen_count)
    token_count, model_width = hidden_states.shape
    head_feats = w_query.shape[1]
    head_width = model_width // H
    head_count = head_feats // head_width
    block_count = token_count // CH
    send_column, column_position, receive_position, position_slot = routing(
        nbr_index, row_index, gen_count, per_device, row_size, capacity
    )
    encoded = encode(nbr_embed, enc_gain, enc_qkv, enc_out)
    row_encoded = lax.all_gather(encoded, "enc", axis=0, tiled=True)
    outgoing = jnp.take(row_encoded, send_column, axis=0)
    incoming = lax.all_to_all(outgoing, "gen", split_axis=0, concat_axis=0, tiled=True)
    slot_encoded = jnp.take(incoming, receive_position, axis=0)
    slot_rows = slot_encoded.reshape(row_size * length, enc_width)
    normed = rms_scale(hidden_states, gain)
    queries = jnp.dot(normed, w_query, preferred_element_type=jnp.float32).astype(jnp.bfloat16)
    queries = queries.reshape(block_count, CH, head_count, head_width)
    keys_all = jnp.dot(slot_rows, w_key, preferred_element_type=jnp.float32).astype(jnp.bfloat16)
    values_all = jnp.dot(slot_rows, w_value, preferred_element_type=jnp.float32).astype(
        jnp.bfloat16
    )
    keys_all = keys_all.reshape(block_count, K * length, head_count, head_width)
    values_all = values_all.reshape(block_count, K * length, head_count, head_width)
    raw_scores, probs_full, probs_low, mixed = attention_parts(queries, keys_all, values_all)
    mixed_rows = mixed.reshape(token_count, head_feats)
    d_mixed = jnp.dot(grad_out, w_out.T, preferred_element_type=jnp.float32).astype(jnp.bfloat16)
    out_term = jnp.dot(mixed_rows.T, grad_out, preferred_element_type=jnp.float32)
    d_keys, d_values = attention_grads(
        queries,
        values_all,
        raw_scores,
        probs_full,
        probs_low,
        d_mixed.reshape(block_count, CH, head_count, head_width),
    )
    d_keys_rows = d_keys.reshape(row_size * length, head_feats)
    d_values_rows = d_values.reshape(row_size * length, head_feats)
    key_term = jnp.dot(slot_rows.T, d_keys_rows, preferred_element_type=jnp.float32)
    value_term = jnp.dot(slot_rows.T, d_values_rows, preferred_element_type=jnp.float32)
    enc_term = jnp.dot(d_keys_rows, w_key.T, preferred_element_type=jnp.float32) + jnp.dot(
        d_values_rows, w_value.T, preferred_element_type=jnp.float32
    )
    enc_term_low = enc_term.astype(jnp.bfloat16).reshape(row_size, length, enc_width)
    returning = jnp.take(enc_term_low, position_slot, axis=0)
    returned = lax.all_to_all(returning, "gen", split_axis=0, concat_axis=0, tiled=True)
    row_grads = jnp.take(returned, column_position, axis=0).astype(jnp.float32)
    grad_encoded = lax.psum_scatter(
        row_grads.astype(jnp.bfloat16), "enc", scatter_dimension=0, tiled=True
    ).astype(jnp.float32)
    grad_w_out, grad_w_key, grad_w_value = (
        lax.psum_scatter(
            out_term.astype(jnp.bfloat16), "gen", scatter_dimension=1, tiled=True
        ).astype(jnp.float32),
        lax.psum_scatter(
            key_term.astype(jnp.bfloat16), "gen", scatter_dimension=0, tiled=True
        ).astype(jnp.float32),
        lax.psum_scatter(
            value_term.astype(jnp.bfloat16), "gen", scatter_dimension=0, tiled=True
        ).astype(jnp.float32),
    )
    return (grad_encoded, grad_w_out, grad_w_key, grad_w_value)


def solution(mesh):
    return jax.shard_map(
        local,
        mesh=mesh,
        in_specs=(
            P("gen", None),
            P("gen", None),
            P(("enc", "gen"), None, None),
            P(),
            P(),
            P(None, "enc"),
            P("enc", None),
            P(None, "enc"),
            P(None, "enc"),
            P(),
            P(),
            P(),
        ),
        out_specs=(
            P(("enc", "gen"), None, None),
            P("enc", "gen"),
            P("gen", "enc"),
            P("gen", "enc"),
        ),
        check_vma=False,
    )
```

profile of v0, /device:TPU:0, one launch (start us, length us, event | category | flops | bytes accessed | tf_op | source)
XLA Modules:
  0.0 657.2 jit_solution(7774443420112423372)
XLA Ops:
  7.2 1.4 fusion.41
  8.6 1.2 fusion.43
  9.8 4.6 fusion.23
  16.9 2.5 fusion.26
  19.5 2.1 convolution_convert_fusion.7
  21.6 1.5 fusion.29
  24.4 33.7 %all-gather.2.cloned.1.call-done = bf16[16,128,1024]{2,1,0:T(8,128)(2,1)} async-done(((bf16[2,128,1024]{2,1,0:T(8,128)(2,1)}), bf16[16,128,1024]{2,1,0:T(8,128)(2,1)}) %all-gather.2.cloned.1.call-update) | async-done | bytes 4194320 | tf_op jit(solution)/shard_map/all_gather | solution.py:121
  58.1 7.1 %gather_fusion = bf16[32,128,1024]{2,1,0:T(8,128)(2,1)} fusion(bf16[16,128,1024]{2,1,0:T(8,128)(2,1)} %all-gather.2.cloned.1.call-done, s32[1024]{0:T(1024)S(1)} %pad_clamp_fusion.3), kind=kCustom, calls=%fused_computation.clone | custom fusion | bytes 16777344 | tf_op jit(solution)/shard_map/jit(_take)/gather | solution.py:122
  65.1 7.5 %broadcast_select_fusion.1 = bf16[32,128,1024]{2,1,0:T(8,128)(2,1)} fusion(bf16[32,128,1024]{2,1,0:T(8,128)(2,1)} %gather_fusion, pred[32]{0:T(512)(128)(4,1)S(1)} %compare_and_fusion.3), kind=kLoop, calls=%fused_computation.12 | loop fusion | flops 4194304 | bytes 16777248 | tf_op jit(solution)/shard_map/jit(_take)/select_n | solution.py:122
  72.6 7.0 %all-to-all-start = ((bf16[32,128,1024]{2,1,0:T(8,128)(2,1)}), bf16[32,128,1024]{2,1,0:T(8,128)(2,1)}, u32[]{:S(2)}, u32[]{:S(2)}) async-start(bf16[32,128,1024]{2,1,0:T(8,128)(2,1)} %broadcast_select_fusion.1), calls=%async_computation | async-start | bytes 16777216 | tf_op jit(solution)/shard_map/all_to_all | solution.py:123
  80.1 3.2 fusion.1
  83.6 4.6 fusion.35
  88.3 5.8 convolution_convert_fusion.6
  94.3 133.0 %all-to-all-done = bf16[32,128,1024]{2,1,0:T(8,128)(2,1)} async-done(((bf16[32,128,1024]{2,1,0:T(8,128)(2,1)}), bf16[32,128,1024]{2,1,0:T(8,128)(2,1)}, u32[]{:S(2)}, u32[]{:S(2)}) %all-to-all-start) | async-done | bytes 8388640 | tf_op jit(solution)/shard_map/all_to_all | solution.py:123
  227.4 6.2 gather_fusion.1
  233.5 2.7 broadcast_select_fusion.3
  236.3 1.9 copy-done.5
  238.2 3.7 convolution_convert_fusion.2
  241.9 2.7 reshape.226
  244.6 6.2 convolution_convert_fusion.3
  250.8 4.0 reshape.224
  254.8 2.2 fusion.19
  257.0 2.2 fusion.22
  259.2 16.0 %convert_bitcast_fusion.1 = bf16[8,256,4,128]{1,3,2,0:T(8,128)(2,1)} fusion(f32[8,4,64,256]{3,2,1,0:T(8,128)} %fusion.19, f32[8,4,64,256]{3,2,1,0:T(8,128)} %get-tuple-element.15, bf16[8,64,4,128]{3,2,1,0:T(4,128)(2,1)S(1)} %reshape.217, f32[8,4,64]{2,1,0:T(4,128)S(1)} %get-tuple-element.14), kind=kOutput, calls=%fused_computation.27 | convolution fusion | flops 142608640 | bytes 6823936 | tf_op jit(solution)/shard_map/bhqk,bqhd->bkhd/dot_general | solution.py:41
  275.2 2.8 copy.80
  278.7 1.3 copy-done.8
  281.0 3.4 convolution_convert_fusion.5
  284.7 2.6 convert_bitcast_fusion
  287.3 1.2 copy.82
  289.2 1.4 copy-done.10
  291.5 3.5 convolution_convert_fusion.4
  295.0 2.6 fusion.38
  298.1 5.7 fusion.81
  303.8 4.3 convolution_convert_fusion
  308.1 8.5 %add_convert_fusion = bf16[2048,1024]{1,0:T(8,128)(2,1)} fusion(f32[2048,1024]{1,0:T(8,128)} %fusion.81, bf16[2048,512]{0,1:T(8,128)(2,1)} %bitcast.96, bf16[1024,512]{1,0:T(8,128)(2,1)S(1)} %copy-done.15), kind=kOutput, calls=%fused_computation.10 | convolution fusion | flops 2151677952 | bytes 15728640 | tf_op jit(solution)/shard_map/dot_general | solution.py:151
  316.6 7.2 %gather_fusion.2 = bf16[32,128,1024]{2,1,0:T(8,128)(2,1)} fusion(bf16[16,128,1024]{2,1,0:T(8,128)(2,1)} %bitcast.84, s32[1024]{0:T(1024)S(1)} %pad_clamp_fusion.1), kind=kCustom, calls=%fused_computation.2.clone | custom fusion | bytes 16777344 | tf_op jit(solution)/shard_map/jit(_take)/gather | solution.py:155
  323.8 7.5 %broadcast_select_fusion = bf16[32,128,1024]{2,1,0:T(8,128)(2,1)} fusion(bf16[32,128,1024]{2,1,0:T(8,128)(2,1)} %gather_fusion.2, pred[32]{0:T(512)(128)(4,1)S(1)} %compare_and_fusion.1), kind=kLoop, calls=%fused_computation.11 | loop fusion | flops 4194304 | bytes 16777248 | tf_op jit(solution)/shard_map/jit(_take)/select_n | solution.py:155
  331.3 11.5 %all-to-all-start.1 = ((bf16[32,128,1024]{2,1,0:T(8,128)(2,1)}), bf16[32,128,1024]{2,1,0:T(8,128)(2,1)}, u32[]{:S(2)}, u32[]{:S(2)}) async-start(bf16[32,128,1024]{2,1,0:T(8,128)(2,1)} %broadcast_select_fusion), calls=%async_computation.1 | async-start | bytes 16777216 | tf_op jit(solution)/shard_map/all_to_all | solution.py:156
  343.0 130.1 %all-to-all-done.1 = bf16[32,128,1024]{2,1,0:T(8,128)(2,1)} async-done(((bf16[32,128,1024]{2,1,0:T(8,128)(2,1)}), bf16[32,128,1024]{2,1,0:T(8,128)(2,1)}, u32[]{:S(2)}, u32[]{:S(2)}) %all-to-all-start.1) | async-done | bytes 8388640 | tf_op jit(solution)/shard_map/all_to_all | solution.py:156
  473.1 6.2 gather_fusion.3
  479.3 4.7 broadcast_select_fusion.2
  484.0 1.6 convert_element_type.136
  485.7 41.9 %reduce-scatter.11.cloned.1.call-done = bf16[64,512]{1,0:T(8,128)(2,1)} async-done(((bf16[1024,512]{1,0:T(8,128)(2,1)}), bf16[64,512]{1,0:T(8,128)(2,1)}) %reduce-scatter.11.cloned.1.call-update) | async-done | bytes 65552 | tf_op jit(solution)/shard_map/reduce_scatter | solution.py:168
  527.6 1.5 convert_element_type.138
  529.1 79.5 %reduce-scatter.7.cloned.1.call-done = bf16[512,256]{1,0:T(8,128)(2,1)} async-done(((bf16[512,4096]{1,0:T(8,128)(2,1)}), bf16[512,256]{1,0:T(8,128)(2,1)}) %reduce-scatter.7.cloned.1.call-update) | async-done | bytes 262160 | tf_op jit(solution)/shard_map/reduce_scatter | solution.py:162
  608.6 1.8 convert_element_type.134
  610.4 38.0 %reduce-scatter.5.cloned.1.call-done = bf16[2,128,1024]{2,1,0:T(8,128)(2,1)} async-done(((bf16[16,128,1024]{2,1,0:T(8,128)(2,1)}), bf16[2,128,1024]{2,1,0:T(8,128)(2,1)}) %reduce-scatter.5.cloned.1.call-update) | async-done | bytes 524304 | tf_op jit(solution)/shard_map/reduce_scatter | solution.py:158
  648.3 2.1 convert_element_type.130
  (83 shorter events, 9.0 us)
Async XLA Ops:
  7.2 14.4 %copy-start = (bf16[1024,1024]{1,0:T(8,128)(2,1)S(1)}, bf16[1024,1024]{1,0:T(8,128)(2,1)}, u32[]{:S(2)}) copy-start(bf16[1024,1024]{1,0:T(8,128)(2,1)} %param.27) | copy-start | bytes 6291460
  7.2 50.9 %all-gather.2.cloned.1.call-start = ((), (), s32[]{:S(2)}) async-start(), calls=%async_computation.6 | async-start | bytes 4718592 | tf_op jit(solution)/shard_map/all_gather | solution.py:121
  19.5 2.1 copy-start.2
  21.6 1.6 copy-start.12
  72.6 10.8 %copy-start.16 = (f32[4096]{0:T(1024)S(1)}, f32[4096]{0:T(1024)}, u32[]{:S(2)}) copy-start(f32[4096]{0:T(1024)} %param.20) | copy-start | bytes 49156
  72.6 154.7 %all-to-all-start = ((bf16[32,128,1024]{2,1,0:T(8,128)(2,1)}), bf16[32,128,1024]{2,1,0:T(8,128)(2,1)}, u32[]{:S(2)}, u32[]{:S(2)}) async-start(bf16[32,128,1024]{2,1,0:T(8,128)(2,1)} %broadcast_select_fusion.1), calls=%async_computation | async-start | bytes 16777216 | tf_op jit(solution)/shard_map/all_to_all | solution.py:123
  79.6 404.4 %reduce-scatter.9.cloned.1.call-start = ((), (), s32[]{:S(2)}) async-start(), calls=%async_computation.9 | async-start | bytes 1114112 | tf_op jit(solution)/shard_map/reduce_scatter | solution.py:165
  80.1 3.5 copy-start.3
  233.5 4.7 copy-start.14
  236.3 1.9 copy-start.5
  254.8 2.2 copy-start.11
  278.0 2.9 copy-start.6
  278.7 1.3 copy-start.8
  284.3 243.3 %reduce-scatter.11.cloned.1.call-start = ((), (), s32[]{:S(2)}) async-start(), calls=%async_computation.10 | async-start | bytes 1114112 | tf_op jit(solution)/shard_map/reduce_scatter | solution.py:168
  288.5 2.9 copy-start.7
  289.2 1.4 copy-start.10
  295.0 313.6 %reduce-scatter.7.cloned.1.call-start = ((), (), s32[]{:S(2)}) async-start(), calls=%async_computation.8 | async-start | bytes 4456448 | tf_op jit(solution)/shard_map/reduce_scatter | solution.py:162
  295.0 3.1 copy-start.9
  295.0 3.1 copy-start.13
  298.1 5.7 copy-start.4
  303.8 4.3 copy-start.15
  331.3 141.8 %all-to-all-start.1 = ((bf16[32,128,1024]{2,1,0:T(8,128)(2,1)}), bf16[32,128,1024]{2,1,0:T(8,128)(2,1)}, u32[]{:S(2)}, u32[]{:S(2)}) async-start(bf16[32,128,1024]{2,1,0:T(8,128)(2,1)} %broadcast_select_fusion), calls=%async_computation.1 | async-start | bytes 16777216 | tf_op jit(solution)/shard_map/all_to_all | solution.py:156
  342.8 305.5 %reduce-scatter.5.cloned.1.call-start = ((), (), s32[]{:S(2)}) async-start(), calls=%async_computation.7 | async-start | bytes 4718592 | tf_op jit(solution)/shard_map/reduce_scatter | solution.py:158
  484.0 166.5 %copy-start.1 = (bf16[1024,1024]{1,0:T(8,128)(2,1)S(1)}, bf16[1024,1024]{1,0:T(8,128)(2,1)}, u32[]{:S(2)}) copy-start(bf16[1024,1024]{1,0:T(8,128)(2,1)} %param.27) | copy-start | bytes 6291460
Sparse Core Ops, SparseCore 0:
  23.3 34.7 all-gather.1
  284.5 121.2 reduce-scatter.8
  409.0 118.6 reduce-scatter.10
  530.8 77.7 reduce-scatter.6
  610.8 37.4 reduce-scatter.4
where the time goes:
time: 663 us; the launch traced here: 657 us
  waiting for transfers between devices  456 us (69%)
  matrix products  82 us (12%)
  local copies, waits for them, and re-layouts  48.9 us (7%)
  other arithmetic  36.3 us (5%)
  starting transfers between devices  19.4 us (3%)
  between operations  14.4 us (2%)
    all_to_all x1, waiting for transfers between devices, local(): lax.all_to_all(outgoing, 'gen', split_axis=0, concat_axis=0, tiled=True)  133 us
    all_to_all x1, waiting for transfers between devices, local(): lax.all_to_all(returning, 'gen', split_axis=0, concat_axis=0, tiled=True)  130 us
    reduce_scatter x1, waiting for transfers between devices, local(): lax.psum_scatter(out_term.astype(jnp.bfloat16), 'gen', scatter_dimension=...  79.5 us
    reduce_scatter x1, waiting for transfers between devices, local(): lax.psum_scatter(value_term.astype(jnp.bfloat16), 'gen', scatter_dimensio...  41.9 us
    reduce_scatter x1, waiting for transfers between devices, local(): lax.psum_scatter(row_grads.astype(jnp.bfloat16), 'enc', scatter_dimension...  38 us
    all_gather x1, waiting for transfers between devices, local(): row_encoded = lax.all_gather(encoded, 'enc', axis=0, tiled=True)  33.7 us
    dot_general x1, matrix products, attention_grads(): jnp.einsum('bhqk,bqhd->bkhd', d_raw, queries, preferred_element_type=jnp....  16 us
  transfers between devices with their start and end apart: 7, of which 6 were waited for; matrix products, arithmetic and copies ran while one was open for 11% of the time, Pallas kernels for 0%

commit v1 on v0

--- a/solution.py
+++ b/solution.py
@@ -118,7 +118,9 @@
         nbr_index, row_index, gen_count, per_device, row_size, capacity
     )
     encoded = encode(nbr_embed, enc_gain, enc_qkv, enc_out)
-    row_encoded = lax.all_gather(encoded, "enc", axis=0, tiled=True)
+    row_encoded = jnp.concatenate(
+        lax.all_to_all(jnp.stack([encoded] * lax.axis_size("enc")), "enc", 0, 0), axis=0
+    )
     outgoing = jnp.take(row_encoded, send_column, axis=0)
     incoming = lax.all_to_all(outgoing, "gen", split_axis=0, concat_axis=0, tiled=True)
     slot_encoded = jnp.take(incoming, receive_position, axis=0)

time: 663 us -> 695 us (1.048)
  waiting for transfers between devices: 456 us -> 482 us
    all_to_all x0 -> x1, waiting for transfers between devices: none -> 48.5 us  [local(): lax.all_to_all(jnp.stack([encoded] * lax.axis_size('enc')), 'enc', 0, 0)]
    all_gather x1 -> x0, waiting for transfers between devices: 33.7 us -> none  [local(): row_encoded = lax.all_gather(encoded, 'enc', axis=0, tiled=True)]
    reduce_scatter x1, waiting for transfers between devices: 41.9 us -> 69 us  [local(): lax.psum_scatter(value_term.astype(jnp.bfloat16), 'gen', scatter_dimensio...]
    all_to_all x1, waiting for transfers between devices: 130 us -> 117 us  [local(): lax.all_to_all(returning, 'gen', split_axis=0, concat_axis=0, tiled=True)]
where the time goes in v1:
time: 695 us; the launch traced here: 688 us
  waiting for transfers between devices  482 us (69%)
  matrix products  81.2 us (12%)
  local copies, waits for them, and re-layouts  51.4 us (7%)
  other arithmetic  36.2 us (5%)
  starting transfers between devices  23.4 us (3%)
  between operations  14.4 us (2%)
    all_to_all x1, waiting for transfers between devices, local(): lax.all_to_all(outgoing, 'gen', split_axis=0, concat_axis=0, tiled=True)  129 us
    all_to_all x1, waiting for transfers between devices, local(): lax.all_to_all(returning, 'gen', split_axis=0, concat_axis=0, tiled=True)  117 us
    reduce_scatter x1, waiting for transfers between devices, local(): lax.psum_scatter(out_term.astype(jnp.bfloat16), 'gen', scatter_dimension=...  79.7 us
    reduce_scatter x1, waiting for transfers between devices, local(): lax.psum_scatter(value_term.astype(jnp.bfloat16), 'gen', scatter_dimensio...  69 us
    all_to_all x1, waiting for transfers between devices, local(): lax.all_to_all(jnp.stack([encoded] * lax.axis_size('enc')), 'enc', 0, 0)  48.5 us
    reduce_scatter x1, waiting for transfers between devices, local(): lax.psum_scatter(row_grads.astype(jnp.bfloat16), 'enc', scatter_dimension...  38 us
    dot_general x1, matrix products, attention_grads(): jnp.einsum('bhqk,bqhd->bkhd', d_raw, queries, preferred_element_type=jnp....  16 us
  transfers between devices with their start and end apart: 7, of which 6 were waited for; matrix products, arithmetic and copies ran while one was open for 11% of the time, Pallas kernels for 0%

profile of v1, /device:TPU:0, one launch (start us, length us, event | category | flops | bytes accessed | tf_op | source)
XLA Modules:
  0.0 688.4 jit_solution(6158156021148098062)
XLA Ops:
  7.2 1.4 fusion.41
  8.6 1.2 fusion.43
  9.8 4.6 fusion.23
  16.9 2.5 fusion.26
  19.5 2.1 convolution_convert_fusion.7
  22.3 2.5 stack.2
  24.8 5.5 all-to-all-start
  31.6 48.5 %all-to-all-done = bf16[8,2,128,1024]{3,2,1,0:T(8,128)(2,1)} async-done(((bf16[8,2,128,1024]{3,2,1,0:T(8,128)(2,1)}), bf16[8,2,128,1024]{3,2,1,0:T(8,128)(2,1)}, u32[]{:S(2)}, u32[]{:S(2)}) %all-to-all-start) | async-done | bytes 4194336 | tf_op jit(solution)/shard_map/all_to_all | solution.py:122
  80.1 7.1 %gather_fusion = bf16[32,128,1024]{2,1,0:T(8,128)(2,1)} fusion(bf16[16,128,1024]{2,1,0:T(8,128)(2,1)} %bitcast.10, s32[1024]{0:T(1024)S(1)} %pad_clamp_fusion.3), kind=kCustom, calls=%fused_computation.clone | custom fusion | bytes 16777344 | tf_op jit(solution)/shard_map/jit(_take)/gather | solution.py:124
  87.2 7.5 %broadcast_select_fusion.1 = bf16[32,128,1024]{2,1,0:T(8,128)(2,1)} fusion(bf16[32,128,1024]{2,1,0:T(8,128)(2,1)} %gather_fusion, pred[32]{0:T(512)(128)(4,1)S(1)} %compare_and_fusion.3), kind=kLoop, calls=%fused_computation.12 | loop fusion | flops 4194304 | bytes 16777248 | tf_op jit(solution)/shard_map/jit(_take)/select_n | solution.py:124
  94.6 7.2 %all-to-all-start.1 = ((bf16[32,128,1024]{2,1,0:T(8,128)(2,1)}), bf16[32,128,1024]{2,1,0:T(8,128)(2,1)}, u32[]{:S(2)}, u32[]{:S(2)}) async-start(bf16[32,128,1024]{2,1,0:T(8,128)(2,1)} %broadcast_select_fusion.1), calls=%async_computation.1 | async-start | bytes 16777216 | tf_op jit(solution)/shard_map/all_to_all | solution.py:125
  102.4 3.2 fusion.1
  105.8 4.6 fusion.35
  110.5 5.8 convolution_convert_fusion.6
  116.6 129.3 %all-to-all-done.1 = bf16[32,128,1024]{2,1,0:T(8,128)(2,1)} async-done(((bf16[32,128,1024]{2,1,0:T(8,128)(2,1)}), bf16[32,128,1024]{2,1,0:T(8,128)(2,1)}, u32[]{:S(2)}, u32[]{:S(2)}) %all-to-all-start.1) | async-done | bytes 8388640 | tf_op jit(solution)/shard_map/all_to_all | solution.py:125
  245.9 6.2 gather_fusion.1
  252.0 2.7 broadcast_select_fusion.3
  254.8 1.9 copy-done.5
  256.7 3.7 convolution_convert_fusion.2
  260.4 2.7 reshape.232
  263.2 6.2 convolution_convert_fusion.3
  269.3 4.0 reshape.230
  273.3 2.2 fusion.19
  275.5 2.2 fusion.22
  277.7 16.0 %convert_bitcast_fusion.1 = bf16[8,256,4,128]{1,3,2,0:T(8,128)(2,1)} fusion(f32[8,4,64,256]{3,2,1,0:T(8,128)} %fusion.19, f32[8,4,64,256]{3,2,1,0:T(8,128)} %get-tuple-element.15, bf16[8,64,4,128]{3,2,1,0:T(4,128)(2,1)S(1)} %reshape.222, f32[8,4,64]{2,1,0:T(4,128)S(1)} %get-tuple-element.14), kind=kOutput, calls=%fused_computation.27 | convolution fusion | flops 142608640 | bytes 6823936 | tf_op jit(solution)/shard_map/bhqk,bqhd->bkhd/dot_general | solution.py:41
  293.8 2.8 copy.61
  297.2 1.3 copy-done.8
  299.5 3.4 convolution_convert_fusion.5
  303.2 2.6 convert_bitcast_fusion
  307.8 1.4 copy-done.10
  310.0 3.5 convolution_convert_fusion.4
  313.6 2.6 fusion.38
  316.7 5.7 fusion.81
  322.3 4.3 convolution_convert_fusion
  326.6 8.5 %add_convert_fusion = bf16[2048,1024]{1,0:T(8,128)(2,1)} fusion(f32[2048,1024]{1,0:T(8,128)} %fusion.81, bf16[2048,512]{0,1:T(8,128)(2,1)} %bitcast.97, bf16[1024,512]{1,0:T(8,128)(2,1)S(1)} %copy-done.15), kind=kOutput, calls=%fused_computation.10 | convolution fusion | flops 2151677952 | bytes 15728640 | tf_op jit(solution)/shard_map/dot_general | solution.py:153
  335.1 7.1 %gather_fusion.2 = bf16[32,128,1024]{2,1,0:T(8,128)(2,1)} fusion(bf16[16,128,1024]{2,1,0:T(8,128)(2,1)} %bitcast.85, s32[1024]{0:T(1024)S(1)} %pad_clamp_fusion.1), kind=kCustom, calls=%fused_computation.2.clone | custom fusion | bytes 16777344 | tf_op jit(solution)/shard_map/jit(_take)/gather | solution.py:157
  342.2 7.5 %broadcast_select_fusion = bf16[32,128,1024]{2,1,0:T(8,128)(2,1)} fusion(bf16[32,128,1024]{2,1,0:T(8,128)(2,1)} %gather_fusion.2, pred[32]{0:T(512)(128)(4,1)S(1)} %compare_and_fusion.1), kind=kLoop, calls=%fused_computation.11 | loop fusion | flops 4194304 | bytes 16777248 | tf_op jit(solution)/shard_map/jit(_take)/select_n | solution.py:157
  349.7 9.8 %all-to-all-start.2 = ((bf16[32,128,1024]{2,1,0:T(8,128)(2,1)}), bf16[32,128,1024]{2,1,0:T(8,128)(2,1)}, u32[]{:S(2)}, u32[]{:S(2)}) async-start(bf16[32,128,1024]{2,1,0:T(8,128)(2,1)} %broadcast_select_fusion), calls=%async_computation.2 | async-start | bytes 16777216 | tf_op jit(solution)/shard_map/all_to_all | solution.py:158
  359.8 117.2 %all-to-all-done.2 = bf16[32,128,1024]{2,1,0:T(8,128)(2,1)} async-done(((bf16[32,128,1024]{2,1,0:T(8,128)(2,1)}), bf16[32,128,1024]{2,1,0:T(8,128)(2,1)}, u32[]{:S(2)}, u32[]{:S(2)}) %all-to-all-start.2) | async-done | bytes 8388640 | tf_op jit(solution)/shard_map/all_to_all | solution.py:158
  477.0 6.2 gather_fusion.3
  483.2 4.7 broadcast_select_fusion.2
  487.9 1.6 convert_element_type.136
  489.5 69.0 %reduce-scatter.11.cloned.1.call-done = bf16[64,512]{1,0:T(8,128)(2,1)} async-done(((bf16[1024,512]{1,0:T(8,128)(2,1)}), bf16[64,512]{1,0:T(8,128)(2,1)}) %reduce-scatter.11.cloned.1.call-update) | async-done | bytes 65552 | tf_op jit(solution)/shard_map/reduce_scatter | solution.py:170
  558.5 1.5 convert_element_type.138
  560.0 79.7 %reduce-scatter.7.cloned.1.call-done = bf16[512,256]{1,0:T(8,128)(2,1)} async-done(((bf16[512,4096]{1,0:T(8,128)(2,1)}), bf16[512,256]{1,0:T(8,128)(2,1)}) %reduce-scatter.7.cloned.1.call-update) | async-done | bytes 262160 | tf_op jit(solution)/shard_map/reduce_scatter | solution.py:164
  639.7 1.8 convert_element_type.134
  641.5 38.0 %reduce-scatter.5.cloned.1.call-done = bf16[2,128,1024]{2,1,0:T(8,128)(2,1)} async-done(((bf16[16,128,1024]{2,1,0:T(8,128)(2,1)}), bf16[2,128,1024]{2,1,0:T(8,128)(2,1)}) %reduce-scatter.5.cloned.1.call-update) | async-done | bytes 524304 | tf_op jit(solution)/shard_map/reduce_scatter | solution.py:160
  679.5 2.1 convert_element_type.130
  (83 shorter events, 10.9 us)
Async XLA Ops:
  7.2 14.4 %copy-start = (bf16[1024,1024]{1,0:T(8,128)(2,1)S(1)}, bf16[1024,1024]{1,0:T(8,128)(2,1)}, u32[]{:S(2)}) copy-start(bf16[1024,1024]{1,0:T(8,128)(2,1)} %param.27) | copy-start | bytes 6291460
  19.5 2.1 copy-start.2
  24.8 5.5 copy-start.12
  24.8 55.3 %all-to-all-start = ((bf16[8,2,128,1024]{3,2,1,0:T(8,128)(2,1)}), bf16[8,2,128,1024]{3,2,1,0:T(8,128)(2,1)}, u32[]{:S(2)}, u32[]{:S(2)}) async-start(bf16[8,2,128,1024]{3,2,1,0:T(8,128)(2,1)} %stack.2), calls=%async_computation | async-start | bytes 8388608 | tf_op jit(solution)/shard_map/all_to_all | solution.py:122
  94.6 11.0 %copy-start.16 = (f32[4096]{0:T(1024)S(1)}, f32[4096]{0:T(1024)}, u32[]{:S(2)}) copy-start(f32[4096]{0:T(1024)} %param.20) | copy-start | bytes 49156
  94.6 151.2 %all-to-all-start.1 = ((bf16[32,128,1024]{2,1,0:T(8,128)(2,1)}), bf16[32,128,1024]{2,1,0:T(8,128)(2,1)}, u32[]{:S(2)}, u32[]{:S(2)}) async-start(bf16[32,128,1024]{2,1,0:T(8,128)(2,1)} %broadcast_select_fusion.1), calls=%async_computation.1 | async-start | bytes 16777216 | tf_op jit(solution)/shard_map/all_to_all | solution.py:125
  101.9 386.0 %reduce-scatter.9.cloned.1.call-start = ((), (), s32[]{:S(2)}) async-start(), calls=%async_computation.9 | async-start | bytes 1114112 | tf_op jit(solution)/shard_map/reduce_scatter | solution.py:167
  102.4 3.5 copy-start.3
  252.0 4.7 copy-start.14
  254.8 1.9 copy-start.5
  273.3 2.2 copy-start.11
  296.5 2.9 copy-start.6
  297.2 1.3 copy-start.8
  302.9 255.7 %reduce-scatter.11.cloned.1.call-start = ((), (), s32[]{:S(2)}) async-start(), calls=%async_computation.10 | async-start | bytes 1114112 | tf_op jit(solution)/shard_map/reduce_scatter | solution.py:170
  307.1 2.9 copy-start.7
  307.8 1.4 copy-start.10
  313.5 326.3 %reduce-scatter.7.cloned.1.call-start = ((), (), s32[]{:S(2)}) async-start(), calls=%async_computation.8 | async-start | bytes 4456448 | tf_op jit(solution)/shard_map/reduce_scatter | solution.py:164
  313.5 3.1 copy-start.9
  313.6 3.1 copy-start.13
  316.6 5.7 copy-start.4
  322.3 4.3 copy-start.15
  349.7 127.3 %all-to-all-start.2 = ((bf16[32,128,1024]{2,1,0:T(8,128)(2,1)}), bf16[32,128,1024]{2,1,0:T(8,128)(2,1)}, u32[]{:S(2)}, u32[]{:S(2)}) async-start(bf16[32,128,1024]{2,1,0:T(8,128)(2,1)} %broadcast_select_fusion), calls=%async_computation.2 | async-start | bytes 16777216 | tf_op jit(solution)/shard_map/all_to_all | solution.py:158
  359.6 319.9 %reduce-scatter.5.cloned.1.call-start = ((), (), s32[]{:S(2)}) async-start(), calls=%async_computation.7 | async-start | bytes 4718592 | tf_op jit(solution)/shard_map/reduce_scatter | solution.py:160
  487.9 193.8 %copy-start.1 = (bf16[1024,1024]{1,0:T(8,128)(2,1)S(1)}, bf16[1024,1024]{1,0:T(8,128)(2,1)}, u32[]{:S(2)}) copy-start(bf16[1024,1024]{1,0:T(8,128)(2,1)} %param.27) | copy-start | bytes 6291460
Sparse Core Ops, SparseCore 0:
  303.0 138.3 reduce-scatter.8
  444.6 113.9 reduce-scatter.10
  561.9 77.8 reduce-scatter.6
  642.0 37.4 reduce-scatter.4
